TPU v7x, 512 devices: a whole 4x8x8 slice. The times are simulated.
512 devices in a mesh: bin: 64 (over z, x, y_hi), grp: 8 (over y_lo, core).
Axes of the slice: x: 4, y: 8 (y_hi: 2, y_lo: 4; y = y_hi * 4 + y_lo), z: 8, core: 2. Of those that a mesh axis runs over, the one named last changes fastest.
Arguments:
- record: bfloat16 [8, 256, 8704], P('grp', 'bin'), may hold values from -60 to 60
- ref_index: int32 [8, 16], P('grp'), may hold values from 0 to 255, as said below
- offsets: int32 [16], replicated, may hold values from 0 to 7680, as said below
Outputs:
- transfer: bfloat16 [512, 2048, 256], P('bin', 'grp')
Inputs may be any that keep to these rules, and one draw needn't show every extreme that they name: `ref_index`: each row lists 16 different channels of its group; every row holds 0 and 255. `offsets`: starts rise; the first is 0, the last is 7680, and neighbours lie 512 // 2 to 768 apart.
All inputs are finite; a program needn't handle non-finite values.
Results may differ from a plain program's by a relative error of at most 0.0095.
Values may be sent and summed in bfloat16 or wider, within the bound.
A program may use at most 64 MiB of HBM per device.

v0:
```python
import math
import jax
import jax.numpy as jnp
from jax import lax
from jax.sharding import PartitionSpec as P

L = 1024
NB = 512
ridge_weight = 0.5


def make_table(seg_len, bins):
    sample_num = lax.iota(jnp.int32, seg_len)[:, None]
    bin_num = lax.iota(jnp.int32, bins)[None, :]
    angles = (sample_num * bin_num % seg_len).astype(jnp.float32) * (2.0 * math.pi / seg_len)
    hann_window = 0.5 - 0.5 * jnp.cos(sample_num.astype(jnp.float32) * (2.0 * math.pi / seg_len))
    return jnp.concatenate(
        [hann_window * jnp.cos(angles), -(hann_window * jnp.sin(angles))], axis=1
    ).astype(jnp.bfloat16)


def transform(chan_rows, starts, dft_table, bin_devices):
    seg_len = dft_table.shape[0]
    pieces = jax.vmap(lambda start_at: lax.dynamic_slice_in_dim(chan_rows, start_at, seg_len, 1))(
        starts
    )
    spectra = jnp.einsum(
        "scn,nk->ksc", pieces, dft_table, preferred_element_type=jnp.float32
    ).astype(jnp.bfloat16)
    bin_total = dft_table.shape[1] // 2
    return spectra.reshape(
        2, bin_devices, bin_total // bin_devices, starts.shape[0], chan_rows.shape[0]
    )


def local(record, ref_index, offsets):
    chan_rows = record[0]
    dft_table = make_table(L, NB)
    bin_devices = lax.axis_size("bin")
    spectra = transform(chan_rows, offsets, dft_table, bin_devices)
    channels = lax.all_to_all(spectra, "bin", split_axis=1, concat_axis=4, tiled=True)[:, 0]
    local_refs = jnp.take(channels, ref_index[0], axis=3)
    references = lax.all_gather(local_refs, "grp", axis=3, tiled=True)
    ref_real = references[0]
    ref_imag = references[1]
    ref_blocks = jnp.stack(
        [
            jnp.concatenate([ref_real, -ref_imag], axis=-1),
            jnp.concatenate([ref_imag, ref_real], axis=-1),
        ]
    )
    bins_here = channels.shape[1]
    group_size = math.gcd(bins_here, 4)
    group_count = bins_here // group_size
    real_order = ref_blocks.shape[-1]

    def solve_group(group_index):
        first_bin = group_index * group_size
        ref_group = lax.dynamic_slice_in_dim(ref_blocks, first_bin, group_size, 1)
        chan_group = lax.dynamic_slice_in_dim(channels, first_bin, group_size, 1)
        cross_part = jnp.einsum(
            "pfsr,pfsc->frc", ref_group, chan_group, preferred_element_type=jnp.float32
        )
        auto_part = jnp.einsum(
            "pfsr,pfsq->frq", ref_group, ref_group, preferred_element_type=jnp.float32
        )
        ridge_term = ridge_weight * jnp.trace(auto_part, axis1=1, axis2=2) / real_order
        factor = jnp.linalg.cholesky(
            auto_part + ridge_term[:, None, None] * jnp.eye(real_order, dtype=jnp.float32)
        )
        transfer_t = jax.scipy.linalg.cho_solve((factor, True), cross_part)
        return jnp.swapaxes(transfer_t, 1, 2).astype(jnp.bfloat16)

    results = lax.map(solve_group, jnp.arange(group_count))
    return results.reshape(bins_here, results.shape[2], results.shape[3])


def solution(mesh):
    placed = (P("grp", "bin", None), P("grp", None), P())
    return jax.shard_map(
        local, mesh=mesh, in_specs=placed, out_specs=P("bin", "grp", None), check_vma=False
    )
```

profile of v0, /device:TPU:1, one launch (start us, length us, event | category | flops | bytes accessed | tf_op | source)
XLA Modules:
  0.0 550.2 jit_solution(7552281096765540275)
XLA Ops:
  0.1 8.9 %multiply_convert_fusion = (bf16[1024,512]{1,0:T(8,128)(2,1)S(1)}, bf16[1024,512]{1,0:T(8,128)(2,1)S(1)}) fusion(f32[1024]{0:T(1024)S(1)} %multiply_subtract_fusion), kind=kLoop, calls=%fused_computation.58 | loop fusion | flops 9961472 | bytes 2101248 | tf_op jit(solution)/shard_map/convert.2
  9.0 32.3 %while.17 = (s32[]{:T(128)}, bf16[4,8704]{1,0:T(4,128)(2,1)}, s32[16,2]{0,1:T(2,128)S(1)}, bf16[16,4,1024]{2,1,0:T(4,128)(2,1)S(1)}, s32[]{:T(128)}) while((s32[]{:T(128)}, bf16[4,8704]{1,0:T(4,128)(2,1)}, s32[16,2]{0,1:T(2,128)S(1)}, bf16[16,4,1024]{2,1,0:T(4,128)(2,1)S(1)}, s32[]{:T(128)}) %tuple.87), condition=%wide.while_cond.1, body=%wide.while_body.1.sunk | while | flops 2 | bytes 16481 | solution.py:24
  9.6 1.4 bitcast_dynamic-update-slice_fusion.4
  11.6 1.4 bitcast_dynamic-update-slice_fusion.4
  13.6 1.4 bitcast_dynamic-update-slice_fusion.4
  15.7 1.4 bitcast_dynamic-update-slice_fusion.4
  17.7 1.4 bitcast_dynamic-update-slice_fusion.4
  19.7 1.4 bitcast_dynamic-update-slice_fusion.4
  21.7 1.4 bitcast_dynamic-update-slice_fusion.4
  23.7 1.4 bitcast_dynamic-update-slice_fusion.4
  25.7 1.4 bitcast_dynamic-update-slice_fusion.4
  27.7 1.4 bitcast_dynamic-update-slice_fusion.4
  29.8 1.4 bitcast_dynamic-update-slice_fusion.4
  31.8 1.4 bitcast_dynamic-update-slice_fusion.4
  33.8 1.4 bitcast_dynamic-update-slice_fusion.4
  35.8 1.4 bitcast_dynamic-update-slice_fusion.4
  37.8 1.4 bitcast_dynamic-update-slice_fusion.4
  39.8 1.4 bitcast_dynamic-update-slice_fusion.4
  42.5 1.8 reshape.166
  44.3 19.6 %all-to-all-start = ((bf16[64,2,512]{2,1,0:T(2,128)(2,1)}), bf16[64,2,512]{2,1,0:T(2,128)(2,1)S(1)}, u32[]{:S(2)}, u32[]{:S(2)}) async-start(bf16[64,2,512]{2,1,0:T(2,128)(2,1)} %reshape.166), calls=%async_computation | async-start | bytes 262144 | tf_op jit(solution)/shard_map/all_to_all | solution.py:41
  63.9 13.6 %all-to-all-done = bf16[64,2,512]{2,1,0:T(2,128)(2,1)S(1)} async-done(((bf16[64,2,512]{2,1,0:T(2,128)(2,1)}), bf16[64,2,512]{2,1,0:T(2,128)(2,1)S(1)}, u32[]{:S(2)}, u32[]{:S(2)}) %all-to-all-start) | async-done | bytes 131104 | tf_op jit(solution)/shard_map/all_to_all | solution.py:41
  77.5 0.7 reshape.167
  79.2 16.7 %all_gather.3 = bf16[2,8,16,128]{2,1,0,3:T(8,128)(2,1)S(1)} all-gather(bf16[2,8,16,16]{2,1,0,3:T(8,128)(2,1)S(1)} %select_bitcast_fusion.1), channel_id=1, replica_groups=mesh['bin'=64,'grp'=8] {'grp'}, dimensions={3}, use_global_device_ids=true | all-gather | bytes 73728 | tf_op jit(solution)/shard_map/all_gather | solution.py:43
  96.6 0.8 copy.60
  97.5 452.7 %while.16 = (s32[]{:T(128)}, bf16[2,4,256,256]{3,2,1,0:T(8,128)(2,1)}, s32[2]{0:T(128)S(1)}, bf16[2,8,16,256]{3,2,1,0:T(8,128)(2,1)S(1)}, bf16[2,8,16,256]{3,2,0...) while((s32[]{:T(128)}, ...), condition=%wide.region_6.7_spmd, body=%wide.region_0.6_spmd.sunk | while | flops 1448117248 | bytes 37234176 | solution.py:74
  100.1 46.9 %custom-call.42 = f32[4,128,128]{2,1,0:T(8,128)S(1)} custom-call(f32[4,128,128]{2,1,0:T(8,128)S(1)} %cholesky.172), custom_call_target="Cholesky" | custom-call | tf_op jit(solution)/shard_map/while/body/eval_jaxpr/jit(cholesky)/cholesky | solution.py:68
  147.1 39.3 %custom-call.43 = f32[4,1,128,128]{2,3,1,0:T(8,128)S(1)} custom-call(f32[4,1,128,128]{3,2,1,0:T(8,128)S(1)} %select_bitcast_fusion.3), custom_call_target="InvertDiagBlocksLowerTriangular" | custom-call | tf_op jit(solution)/shard_map/while/body/eval_jaxpr/jit(cholesky)/cholesky | solution.py:68
  186.9 0.7 convolution_subtract_fusion.6
  187.5 46.9 %custom-call.44 = f32[4,128,128]{2,1,0:T(8,128)S(1)} custom-call(f32[4,128,128]{2,1,0:T(8,128)S(1)} %convolution_subtract_fusion.6), custom_call_target="Cholesky" | custom-call | tf_op jit(solution)/shard_map/while/body/eval_jaxpr/jit(cholesky)/cholesky | solution.py:68
  235.1 3.9 while.18
  235.7 1.3 bitcast_dynamic-update-slice_fusion.5
  237.7 1.3 bitcast_dynamic-update-slice_fusion.5
  239.0 78.6 %custom-call.46 = f32[4,2,128,128]{2,3,1,0:T(8,128)S(1)} custom-call(f32[4,2,128,128]{3,2,1,0:T(8,128)S(1)} %bitcast.144), custom_call_target="InvertDiagBlocksLowerTriangular" | custom-call | tf_op jit(solution)/shard_map/while/body/eval_jaxpr/jit(_cho_solve)/vmap()/triangular_solve | solution.py:71
  318.0 0.6 fusion.71
  320.4 0.6 convolution_subtract_fusion.8
  321.9 1.0 copy-done
  323.0 1.0 copy-done.1
  326.3 46.9 %custom-call.42 = f32[4,128,128]{2,1,0:T(8,128)S(1)} custom-call(f32[4,128,128]{2,1,0:T(8,128)S(1)} %cholesky.172), custom_call_target="Cholesky" | custom-call | tf_op jit(solution)/shard_map/while/body/eval_jaxpr/jit(cholesky)/cholesky | solution.py:68
  373.4 39.3 %custom-call.43 = f32[4,1,128,128]{2,3,1,0:T(8,128)S(1)} custom-call(f32[4,1,128,128]{3,2,1,0:T(8,128)S(1)} %select_bitcast_fusion.3), custom_call_target="InvertDiagBlocksLowerTriangular" | custom-call | tf_op jit(solution)/shard_map/while/body/eval_jaxpr/jit(cholesky)/cholesky | solution.py:68
  413.1 0.7 convolution_subtract_fusion.6
  413.8 46.9 %custom-call.44 = f32[4,128,128]{2,1,0:T(8,128)S(1)} custom-call(f32[4,128,128]{2,1,0:T(8,128)S(1)} %convolution_subtract_fusion.6), custom_call_target="Cholesky" | custom-call | tf_op jit(solution)/shard_map/while/body/eval_jaxpr/jit(cholesky)/cholesky | solution.py:68
  461.3 3.9 while.18
  462.0 1.3 bitcast_dynamic-update-slice_fusion.5
  463.9 1.3 bitcast_dynamic-update-slice_fusion.5
  465.3 78.6 %custom-call.46 = f32[4,2,128,128]{2,3,1,0:T(8,128)S(1)} custom-call(f32[4,2,128,128]{3,2,1,0:T(8,128)S(1)} %bitcast.144), custom_call_target="InvertDiagBlocksLowerTriangular" | custom-call | tf_op jit(solution)/shard_map/while/body/eval_jaxpr/jit(_cho_solve)/vmap()/triangular_solve | solution.py:71
  546.7 0.6 convolution_subtract_fusion.8
  548.2 1.0 copy-done
  549.2 1.0 copy-done.1
  (132 shorter events, 27.9 us)
Async XLA Ops:
  0.1 8.9 %copy-start.2 = (s32[16]{0:T(128)S(1)}, s32[16]{0:T(128)}, u32[]{:S(2)}) copy-start(s32[16]{0:T(128)} %param.7) | copy-start | bytes 196
  42.5 21.4 %copy-start.3 = (s32[1,16]{1,0:T(1,128)S(1)}, s32[1,16]{1,0:T(1,128)}, u32[]{:S(2)}) copy-start(s32[1,16]{1,0:T(1,128)} %param.6) | copy-start | bytes 196
  44.3 33.2 %all-to-all-start = ((bf16[64,2,512]{2,1,0:T(2,128)(2,1)}), bf16[64,2,512]{2,1,0:T(2,128)(2,1)S(1)}, u32[]{:S(2)}, u32[]{:S(2)}) async-start(bf16[64,2,512]{2,1,0:T(2,128)(2,1)} %reshape.166), calls=%async_computation | async-start | bytes 262144 | tf_op jit(solution)/shard_map/all_to_all | solution.py:41
  321.7 1.2 copy-start
  322.9 1.0 copy-start.1
  547.9 1.2 copy-start
  549.2 1.0 copy-start.1
where the time goes:
time: 552 us; the launch traced here: 550 us
  other arithmetic  435 us (79%)
  local copies, waits for them, and re-layouts  52.2 us (9%)
  starting transfers between devices  19.6 us (4%)
  blocking collectives  16.7 us (3%)
  waiting for transfers between devices  13.6 us (2%)
  matrix products  11.5 us (2%)
    another operation x20, other arithmetic, solve_group(): jnp.linalg.cholesky(auto_part + ridge_term[:, None, None] * jnp.eye(real_...  267 us
    another operation x8, other arithmetic, solve_group(): transfer_t = jax.scipy.linalg.cho_solve((factor, True), cross_part)  158 us
    gather x48, local copies, waits for them, and re-layouts  32.2 us
    all_to_all x1, starting transfers between devices, local(): lax.all_to_all(spectra, 'bin', split_axis=1, concat_axis=4, tiled=True)  19.6 us
    all_gather x1, blocking collectives, local(): references = lax.all_gather(local_refs, 'grp', axis=3, tiled=True)  16.7 us
    all_to_all x1, waiting for transfers between devices, local(): lax.all_to_all(spectra, 'bin', split_axis=1, concat_axis=4, tiled=True)  13.6 us
  transfers between devices with their start and end apart: 1, of which 1 were waited for; matrix products, arithmetic and copies ran while one was open for 0% of the time, Pallas kernels for 0%

commit v1 on v0

--- a/solution.py
+++ b/solution.py
@@ -38,7 +38,10 @@
     dft_table = make_table(L, NB)
     bin_devices = lax.axis_size("bin")
     spectra = transform(chan_rows, offsets, dft_table, bin_devices)
-    channels = lax.all_to_all(spectra, "bin", split_axis=1, concat_axis=4, tiled=True)[:, 0]
+    channels = jnp.concatenate(
+        lax.all_to_all(jnp.stack(jnp.split(spectra, lax.axis_size("bin"), axis=1)), "bin", 0, 0),
+        axis=4,
+    )[:, 0]
     local_refs = jnp.take(channels, ref_index[0], axis=3)
     references = lax.all_gather(local_refs, "grp", axis=3, tiled=True)
     ref_real = references[0]

time: 552 us -> 553 us (level)
  no operation moved by 1% of the time
where the time goes in v1:
time: 553 us; the launch traced here: 552 us
  other arithmetic  435 us (79%)
  local copies, waits for them, and re-layouts  53.4 us (10%)
  starting transfers between devices  19.6 us (4%)
  blocking collectives  16.7 us (3%)
  waiting for transfers between devices  13.6 us (2%)
  matrix products  11.5 us (2%)
    another operation x20, other arithmetic, solve_group(): jnp.linalg.cholesky(auto_part + ridge_term[:, None, None] * jnp.eye(real_...  267 us
    another operation x8, other arithmetic, solve_group(): transfer_t = jax.scipy.linalg.cho_solve((factor, True), cross_part)  158 us
    gather x48, local copies, waits for them, and re-layouts  32.2 us
    all_to_all x1, starting transfers between devices, local(): lax.all_to_all(jnp.stack(jnp.split(spectra, lax.axis_size('bin'), axis=1)...  19.6 us
    all_gather x1, blocking collectives, local(): references = lax.all_gather(local_refs, 'grp', axis=3, tiled=True)  16.7 us
    all_to_all x1, waiting for transfers between devices, local(): lax.all_to_all(jnp.stack(jnp.split(spectra, lax.axis_size('bin'), axis=1)...  13.6 us
  transfers between devices with their start and end apart: 1, of which 1 were waited for; matrix products, arithmetic and copies ran while one was open for 0% of the time, Pallas kernels for 0%

profile of v1, /device:TPU:1, one launch (start us, length us, event | category | flops | bytes accessed | tf_op | source)
XLA Modules:
  0.0 551.7 jit_solution(8271797535921330326)
XLA Ops:
  0.1 8.9 %multiply_convert_fusion = (bf16[1024,512]{1,0:T(8,128)(2,1)S(1)}, bf16[1024,512]{1,0:T(8,128)(2,1)S(1)}) fusion(f32[1024]{0:T(1024)S(1)} %multiply_subtract_fusion), kind=kLoop, calls=%fused_computation.58 | loop fusion | flops 9961472 | bytes 2101248 | tf_op jit(solution)/shard_map/convert.2
  9.0 32.3 %while.17 = (s32[]{:T(128)}, bf16[4,8704]{1,0:T(4,128)(2,1)}, s32[16,2]{0,1:T(2,128)S(1)}, bf16[16,4,1024]{2,1,0:T(4,128)(2,1)S(1)}, s32[]{:T(128)}) while((s32[]{:T(128)}, bf16[4,8704]{1,0:T(4,128)(2,1)}, s32[16,2]{0,1:T(2,128)S(1)}, bf16[16,4,1024]{2,1,0:T(4,128)(2,1)S(1)}, s32[]{:T(128)}) %tuple.88), condition=%wide.while_cond.1, body=%wide.while_body.1.sunk | while | flops 2 | bytes 16481 | solution.py:24
  9.6 1.4 bitcast_dynamic-update-slice_fusion.4
  11.6 1.4 bitcast_dynamic-update-slice_fusion.4
  13.6 1.4 bitcast_dynamic-update-slice_fusion.4
  15.7 1.4 bitcast_dynamic-update-slice_fusion.4
  17.7 1.4 bitcast_dynamic-update-slice_fusion.4
  19.7 1.4 bitcast_dynamic-update-slice_fusion.4
  21.7 1.4 bitcast_dynamic-update-slice_fusion.4
  23.7 1.4 bitcast_dynamic-update-slice_fusion.4
  25.7 1.4 bitcast_dynamic-update-slice_fusion.4
  27.7 1.4 bitcast_dynamic-update-slice_fusion.4
  29.8 1.4 bitcast_dynamic-update-slice_fusion.4
  31.8 1.4 bitcast_dynamic-update-slice_fusion.4
  33.8 1.4 bitcast_dynamic-update-slice_fusion.4
  35.8 1.4 bitcast_dynamic-update-slice_fusion.4
  37.8 1.4 bitcast_dynamic-update-slice_fusion.4
  39.8 1.4 bitcast_dynamic-update-slice_fusion.4
  43.8 1.8 reshape.169
  45.6 19.6 %all-to-all-start = ((bf16[64,2,512]{2,1,0:T(2,128)(2,1)}), bf16[64,2,512]{2,1,0:T(2,128)(2,1)S(1)}, u32[]{:S(2)}, u32[]{:S(2)}) async-start(bf16[64,2,512]{2,1,0:T(2,128)(2,1)} %reshape.169), calls=%async_computation | async-start | bytes 262144 | tf_op jit(solution)/shard_map/all_to_all | solution.py:42
  65.3 13.6 %all-to-all-done = bf16[64,2,512]{2,1,0:T(2,128)(2,1)S(1)} async-done(((bf16[64,2,512]{2,1,0:T(2,128)(2,1)}), bf16[64,2,512]{2,1,0:T(2,128)(2,1)S(1)}, u32[]{:S(2)}, u32[]{:S(2)}) %all-to-all-start) | async-done | bytes 131104 | tf_op jit(solution)/shard_map/all_to_all | solution.py:42
  78.8 0.7 reshape.170
  80.9 16.7 %all_gather.3 = bf16[2,8,16,128]{2,1,0,3:T(8,128)(2,1)S(1)} all-gather(bf16[2,8,16,16]{2,1,0,3:T(8,128)(2,1)S(1)} %select_bitcast_fusion.1), channel_id=1, replica_groups=mesh['bin'=64,'grp'=8] {'grp'}, dimensions={3}, use_global_device_ids=true | all-gather | bytes 73728 | tf_op jit(solution)/shard_map/all_gather | solution.py:46
  97.6 0.7 copy.398
  99.0 452.7 %while.16 = (s32[]{:T(128)}, bf16[2,4,256,256]{3,2,1,0:T(8,128)(2,1)}, s32[2]{0:T(128)S(1)}, bf16[2,8,16,256]{3,2,1,0:T(8,128)(2,1)S(1)}, bf16[2,8,16,256]{3,2,0...) while((s32[]{:T(128)}, ...), condition=%wide.region_6.7_spmd, body=%wide.region_0.6_spmd.sunk | while | flops 1448117248 | bytes 37234176 | solution.py:77
  101.6 46.9 %custom-call.44 = f32[4,128,128]{2,1,0:T(8,128)S(1)} custom-call(f32[4,128,128]{2,1,0:T(8,128)S(1)} %cholesky.172), custom_call_target="Cholesky" | custom-call | tf_op jit(solution)/shard_map/while/body/eval_jaxpr/jit(cholesky)/cholesky | solution.py:71
  148.6 39.3 %custom-call.45 = f32[4,1,128,128]{2,3,1,0:T(8,128)S(1)} custom-call(f32[4,1,128,128]{3,2,1,0:T(8,128)S(1)} %select_bitcast_fusion.3), custom_call_target="InvertDiagBlocksLowerTriangular" | custom-call | tf_op jit(solution)/shard_map/while/body/eval_jaxpr/jit(cholesky)/cholesky | solution.py:71
  188.4 0.7 convolution_subtract_fusion.6
  189.0 46.9 %custom-call.46 = f32[4,128,128]{2,1,0:T(8,128)S(1)} custom-call(f32[4,128,128]{2,1,0:T(8,128)S(1)} %convolution_subtract_fusion.6), custom_call_target="Cholesky" | custom-call | tf_op jit(solution)/shard_map/while/body/eval_jaxpr/jit(cholesky)/cholesky | solution.py:71
  236.6 3.9 while.18
  237.2 1.3 bitcast_dynamic-update-slice_fusion.5
  239.2 1.3 bitcast_dynamic-update-slice_fusion.5
  240.5 78.6 %custom-call.48 = f32[4,2,128,128]{2,3,1,0:T(8,128)S(1)} custom-call(f32[4,2,128,128]{3,2,1,0:T(8,128)S(1)} %bitcast.583), custom_call_target="InvertDiagBlocksLowerTriangular" | custom-call | tf_op jit(solution)/shard_map/while/body/eval_jaxpr/jit(_cho_solve)/vmap()/triangular_solve | solution.py:74
  321.9 0.6 convolution_subtract_fusion.8
  323.4 1.0 copy-done
  324.5 1.0 copy-done.1
  327.8 46.9 %custom-call.44 = f32[4,128,128]{2,1,0:T(8,128)S(1)} custom-call(f32[4,128,128]{2,1,0:T(8,128)S(1)} %cholesky.172), custom_call_target="Cholesky" | custom-call | tf_op jit(solution)/shard_map/while/body/eval_jaxpr/jit(cholesky)/cholesky | solution.py:71
  374.9 39.3 %custom-call.45 = f32[4,1,128,128]{2,3,1,0:T(8,128)S(1)} custom-call(f32[4,1,128,128]{3,2,1,0:T(8,128)S(1)} %select_bitcast_fusion.3), custom_call_target="InvertDiagBlocksLowerTriangular" | custom-call | tf_op jit(solution)/shard_map/while/body/eval_jaxpr/jit(cholesky)/cholesky | solution.py:71
  414.6 0.7 convolution_subtract_fusion.6
  415.3 46.9 %custom-call.46 = f32[4,128,128]{2,1,0:T(8,128)S(1)} custom-call(f32[4,128,128]{2,1,0:T(8,128)S(1)} %convolution_subtract_fusion.6), custom_call_target="Cholesky" | custom-call | tf_op jit(solution)/shard_map/while/body/eval_jaxpr/jit(cholesky)/cholesky | solution.py:71
  462.8 3.9 while.18
  463.5 1.3 bitcast_dynamic-update-slice_fusion.5
  465.4 1.3 bitcast_dynamic-update-slice_fusion.5
  466.7 78.6 %custom-call.48 = f32[4,2,128,128]{2,3,1,0:T(8,128)S(1)} custom-call(f32[4,2,128,128]{3,2,1,0:T(8,128)S(1)} %bitcast.583), custom_call_target="InvertDiagBlocksLowerTriangular" | custom-call | tf_op jit(solution)/shard_map/while/body/eval_jaxpr/jit(_cho_solve)/vmap()/triangular_solve | solution.py:74
  547.0 0.6 fusion.72
  548.2 0.6 convolution_subtract_fusion.8
  549.7 1.0 copy-done
  550.7 1.0 copy-done.1
  (196 shorter events, 29.2 us)
Async XLA Ops:
  0.1 8.9 %copy-start.2 = (s32[16]{0:T(128)S(1)}, s32[16]{0:T(128)}, u32[]{:S(2)}) copy-start(s32[16]{0:T(128)} %param.7) | copy-start | bytes 196
  43.8 21.4 %copy-start.3 = (s32[1,16]{1,0:T(1,128)S(1)}, s32[1,16]{1,0:T(1,128)}, u32[]{:S(2)}) copy-start(s32[1,16]{1,0:T(1,128)} %param.6) | copy-start | bytes 196
  45.6 33.2 %all-to-all-start = ((bf16[64,2,512]{2,1,0:T(2,128)(2,1)}), bf16[64,2,512]{2,1,0:T(2,128)(2,1)S(1)}, u32[]{:S(2)}, u32[]{:S(2)}) async-start(bf16[64,2,512]{2,1,0:T(2,128)(2,1)} %reshape.169), calls=%async_computation | async-start | bytes 262144 | tf_op jit(solution)/shard_map/all_to_all | solution.py:42
  323.2 1.2 copy-start
  324.4 1.0 copy-start.1
  549.4 1.2 copy-start
  550.7 1.0 copy-start.1
